TPU v7x, 32 devices: a whole 2x2x4 slice. The times are simulated.
32 devices in a mesh: ctx: 8 (over z, core), head: 4 (over y, x).
Axes of the slice: x: 2, y: 2, z: 4, core: 2. Of those that a mesh axis runs over, the one named last changes fastest.
Arguments:
- q_latent: bfloat16 [1024, 1536], P('ctx', 'head'), may hold values from -72 to 72
- latent_cache: bfloat16 [1024, 576], P('ctx'), may hold values from -6 to 6
- w_q_up: bfloat16 [1536, 3072], P(None, 'head'), may hold values from -0.15625 to 0.15625
- w_kv_up: bfloat16 [512, 4096], P(None, 'head'), may hold values from -0.25 to 0.25
- w_out: bfloat16 [2048, 7168], P('head', 'ctx'), may hold values from -1 to 1
- token_pos: int32 [1024], P('ctx'), may hold values from 0 to 1023, as said below
- start_offset: int32 [1], replicated, may hold values from 0 to 65535
Outputs:
- layer_out: bfloat16 [1024, 7168], P('ctx', 'head')
Inputs may be any that keep to these rules, and one draw needn't show every extreme that they name: `token_pos`: a permutation of 0 to 1023; the 128 tokens of each index of ctx hold consecutive positions in increasing order.
All inputs are finite; a program needn't handle non-finite values.
Results may differ from a plain program's by a relative error of at most 0.035.
Values may be sent and summed in bfloat16 or wider, within the bound.
A program may use at most 64 MiB of HBM per device.

v0:
```python
import jax
import jax.numpy as jnp
from jax import lax
from jax.sharding import PartitionSpec as P

KVL = 512
NOPE = 128
ROPE = 64
VDIM = 128


negative_fill = -1e30
softmax_scale = 0.135
rope_base = 10000.0


def rotate(values, angle):
    half = ROPE // 2
    cosine = jnp.cos(angle)
    sine = jnp.sin(angle)
    first = values[..., :half]
    second = values[..., half:]
    return jnp.concatenate(
        [first * cosine - second * sine, first * sine + second * cosine], axis=-1
    )


def shards(q_latent, latent_cache, w_q_up, w_kv_up, w_out, token_pos, start_offset):
    features = lax.all_gather(q_latent, "head", axis=1, tiled=True)
    row_count = features.shape[0]
    head_count = w_q_up.shape[1] // (NOPE + ROPE)
    query = jnp.dot(features, w_q_up, preferred_element_type=jnp.float32).reshape(
        row_count, head_count, NOPE + ROPE
    )
    absolute = (token_pos + start_offset[0]).astype(jnp.float32)
    freqs = rope_base ** (-jnp.arange(ROPE // 2, dtype=jnp.float32) * 2.0 / ROPE)
    angle = absolute[:, None, None] * freqs[None, None, :]
    query_nope = query[..., :NOPE].astype(jnp.bfloat16)
    query_rope = rotate(query[..., NOPE:], angle).astype(jnp.bfloat16)
    kv_weights = w_kv_up.reshape(KVL, head_count, NOPE + VDIM)
    query_main = jnp.einsum(
        "rhn,chn->rhc", query_nope, kv_weights[:, :, :NOPE], preferred_element_type=jnp.float32
    ).astype(jnp.bfloat16)
    value_width = KVL

    def attend(carry, block, key_pos):
        maxima, totals, accum = carry
        latent = block[:, :KVL]
        key_rope = block[:, KVL:]
        scores = jnp.einsum("rhd,kd->hrk", query_rope, key_rope, preferred_element_type=jnp.float32)
        scores = scores + jnp.einsum(
            "rhc,kc->hrk", query_main, latent, preferred_element_type=jnp.float32
        )
        visible = key_pos[None, None, :] <= token_pos[None, :, None]
        scores = jnp.where(visible, scores * softmax_scale, negative_fill)
        new_max = jnp.maximum(maxima, jnp.max(scores, axis=-1))
        weights = jnp.where(visible, jnp.exp(scores - new_max[..., None]), 0.0)
        factor = jnp.exp(maxima - new_max)
        totals = totals * factor + jnp.sum(weights, axis=-1)
        rounded = weights.astype(jnp.bfloat16)
        addition = jnp.einsum("hrk,kc->hrc", rounded, latent, preferred_element_type=jnp.float32)
        return (new_max, totals, accum * factor[..., None] + addition)

    def visit(carry, block, key_pos):
        return attend(carry, block, key_pos)

    initial = (
        jnp.full((head_count, row_count), negative_fill, jnp.float32),
        jnp.zeros((head_count, row_count), jnp.float32),
        jnp.zeros((head_count, row_count, value_width), jnp.float32),
    )
    carry = initial
    block = lax.all_gather(latent_cache, "ctx", axis=0, tiled=True)
    key_pos = lax.all_gather(token_pos, "ctx", axis=0, tiled=True)
    length = block.shape[0]
    count = length // 512

    def scan_step(state, inputs):
        return (visit(state, inputs[0], inputs[1]), None)

    carry, unused = lax.scan(
        scan_step, carry, (block.reshape(count, 512, block.shape[1]), key_pos.reshape(count, 512))
    )
    maxima, totals, accum = carry
    normed = accum / totals[..., None]
    heads_out = jnp.einsum(
        "hrc,chv->rhv",
        normed.astype(jnp.bfloat16),
        kv_weights[:, :, NOPE:],
        preferred_element_type=jnp.float32,
    ).astype(jnp.bfloat16)
    attention = heads_out.reshape(row_count, head_count * VDIM)
    partial_value = jnp.dot(
        attention,
        lax.all_gather(w_out, "ctx", axis=1, tiled=True),
        preferred_element_type=jnp.float32,
    )
    summed = lax.psum_scatter(
        partial_value.astype(jnp.bfloat16), "head", scatter_dimension=1, tiled=True
    )
    return summed


def solution(mesh):
    in_specs = (
        P("ctx", "head"),
        P("ctx", None),
        P(None, "head"),
        P(None, "head"),
        P("head", "ctx"),
        P("ctx"),
        P(),
    )
    out_specs = P("ctx", "head")
    return jax.shard_map(shards, mesh=mesh, in_specs=in_specs, out_specs=out_specs, check_vma=False)
```

profile of v0, /device:TPU:0, one launch (start us, length us, event | category | flops | bytes accessed | tf_op | source)
XLA Modules:
  0.0 153.7 jit_solution(13519243460815425323)
XLA Ops:
  6.5 0.7 all-gather.4.cloned.1.call-update
  7.3 0.7 all-gather.6.cloned.1.call-update
  8.7 1.5 copy.35
  10.3 13.6 %all-gather = s32[8,1,128]{2,1,0:T(1,128)S(1)} all-gather(s32[1,1,128]{2,1,0:T(1,128)S(1)} %bitcast.58), channel_id=1, replica_groups=mesh['ctx'=8,'head'=4] {'ctx'}, dimensions={0}, use_global_device_ids=true | all-gather | bytes 4608 | tf_op jit(solution)/shard_map/all_gather | solution.py:74
  23.8 0.6 broadcast.97
  24.4 0.7 reduce.3
  25.1 11.2 %all_gather.14 = bf16[128,1536]{1,0:T(8,128)(2,1)S(1)} all-gather(bf16[128,384]{1,0:T(8,128)(2,1)} %param.9), channel_id=1, replica_groups=mesh['ctx'=8,'head'=4] {'head'}, dimensions={1}, use_global_device_ids=true | all-gather | bytes 491520 | tf_op jit(solution)/shard_map/all_gather | solution.py:29
  36.5 1.0 fusion.16
  37.6 1.2 fusion.12
  38.8 2.4 %copy.49 = bf16[72,2,8,512]{3,2,0,1:T(8,128)(2,1)} copy(bf16[72,2,8,512]{3,2,1,0:T(8,128)(2,1)} %bitcast.55) | data formatting | bytes 2359296 | tf_op jit(solution)/shard_map/reshape | solution.py:82
  41.2 11.1 %while.15 = (s32[]{:T(128)}, f32[4,128]{1,0:T(4,128)S(1)}, f32[4,128]{1,0:T(4,128)S(1)}, f32[4,128,512]{2,1,0:T(8,128)}, s32[2,512]{1,0:T(2,128)S(1)}, /*index=5...) while((s32[]{:T(128)}, f32[4,128]{1,0:T(4,128)S(1)}, ...), condition=%wide.region_3.4_spmd.clone, body=%wide.region_0.3_spmd.clone.sunk | while | flops 573901312 | bytes 14983901 | solution.py:81
  41.2 1.2 dynamic-slice_bitcast_fusion.2
  42.8 0.4 copy-done.1
  43.2 0.5 fusion.34
  44.0 2.6 %convolution_add_fusion.3 = f32[4,128,512]{2,1,0:T(8,128)} fusion(f32[4,128,512]{2,1,0:T(8,128)} %get-tuple-element.215, f32[4,128,512]{1,2,0:T(8,128)S(1)} %get-tuple-element.198, f32[4,128]{1,0:T(4,128)S(1)} %get-tuple-element.200, f32[4,128]{1,0:T(4,128)S(1)} %select_maximum_fusion.2, pred[]{:T(512)S(6)} %compare.3, ...), kind=kOutput, calls=%fused_computation.clone.1 | convolution fusion | flops 270008320 | bytes 3739649 | tf_op jit(solution)/shard_map/while/body/eval_jaxpr/hrk,kc->hrc/dot_general | solution.py:61
  46.6 1.2 dynamic-slice_bitcast_fusion.2
  47.8 0.3 fusion.33
  48.3 0.4 copy-done.1
  48.7 0.5 fusion.34
  49.4 2.9 %convolution_add_fusion.3 = f32[4,128,512]{2,1,0:T(8,128)} fusion(f32[4,128,512]{2,1,0:T(8,128)} %get-tuple-element.215, f32[4,128,512]{1,2,0:T(8,128)S(1)} %get-tuple-element.198, f32[4,128]{1,0:T(4,128)S(1)} %get-tuple-element.200, f32[4,128]{1,0:T(4,128)S(1)} %select_maximum_fusion.2, pred[]{:T(512)S(6)} %compare.3, ...), kind=kOutput, calls=%fused_computation.clone.1 | convolution fusion | flops 270008320 | bytes 3739649 | tf_op jit(solution)/shard_map/while/body/eval_jaxpr/hrk,kc->hrc/dot_general | solution.py:61
  52.3 1.8 %convolution_convert_fusion.2 = bf16[4,128,128]{1,2,0:T(8,128)(2,1)S(1)} fusion(bf16[512,4,256]{0,2,1:T(8,128)(2,1)} %bitcast.52, f32[4,128,512]{2,1,0:T(8,128)} %get-tuple-element.248, f32[4,128]{1,0:T(4,128)S(1)} %get-tuple-element.247), kind=kOutput, calls=%fused_computation.27 | convolution fusion | flops 67698688 | bytes 1705984 | tf_op jit(solution)/shard_map/hrc,chv->rhv/dot_general | solution.py:86
  54.1 55.7 %all-gather.6.cloned.1.call-done = bf16[512,7168]{1,0:T(8,128)(2,1)} async-done(((bf16[512,896]{1,0:T(8,128)(2,1)}), bf16[512,7168]{1,0:T(8,128)(2,1)}) %all-gather.6.cloned.1.call-update) | async-done | bytes 7340048 | tf_op jit(solution)/shard_map/all_gather | solution.py:95
  109.8 5.5 %convolution_convert_fusion = bf16[128,7168]{1,0:T(8,128)(2,1)} fusion(bf16[128,512]{0,1:T(8,128)(2,1)S(1)} %bitcast.56, bf16[512,7168]{1,0:T(8,128)(2,1)} %all-gather.6.cloned.1.call-done), kind=kOutput, calls=%fused_computation.23 | convolution fusion | flops 940441600 | bytes 9306112 | tf_op jit(solution)/shard_map/dot_general | solution.py:93
  115.4 31.7 %reduce-scatter.2.cloned.1.call-done = bf16[128,1792]{1,0:T(8,128)(2,1)} async-done(((bf16[128,7168]{1,0:T(8,128)(2,1)}), bf16[128,1792]{1,0:T(8,128)(2,1)}) %reduce-scatter.2.cloned.1.call-update) | async-done | bytes 458768 | tf_op jit(solution)/shard_map/reduce_scatter | solution.py:98
  (43 shorter events, 1.4 us)
Async XLA Ops:
  6.5 30.0 %copy-start = (bf16[1536,768]{1,0:T(8,128)(2,1)S(1)}, bf16[1536,768]{1,0:T(8,128)(2,1)}, u32[]{:S(2)}) copy-start(bf16[1536,768]{1,0:T(8,128)(2,1)} %param.11) | copy-start | bytes 7077892
  6.5 3.7 %copy-start.4 = (s32[128]{0:T(128)S(1)}, s32[128]{0:T(128)}, u32[]{:S(2)}) copy-start(s32[128]{0:T(128)} %param.14) | copy-start | bytes 1540
  6.5 32.2 %all-gather.4.cloned.1.call-start = ((), (), s32[]{:S(2)}) async-start(), calls=%async_computation.1 | async-start | bytes 1327104 | tf_op jit(solution)/shard_map/all_gather | solution.py:73
  7.3 102.6 %all-gather.6.cloned.1.call-start = ((), (), s32[]{:S(2)}) async-start(), calls=%async_computation.2 | async-start | bytes 8257536 | tf_op jit(solution)/shard_map/all_gather | solution.py:95
  8.0 139.1 %reduce-scatter.2.cloned.1.call-start = ((), (), s32[]{:S(2)}) async-start(), calls=%async_computation.3 | async-start | bytes 2293760 | tf_op jit(solution)/shard_map/reduce_scatter | solution.py:98
  10.2 28.5 %copy-start.3 = (bf16[512,1024]{0,1:T(8,128)(2,1)}, bf16[512,1024]{0,1:T(8,128)(2,1)S(1)}, u32[]{:S(2)}) copy-start(bf16[512,1024]{0,1:T(8,128)(2,1)S(1)} %copy.35) | copy-start | bytes 3145732
  41.2 2.0 %copy-start.2 = (bf16[128,4,512]{2,0,1:T(8,128)(2,1)S(1)}, bf16[128,4,512]{2,0,1:T(8,128)(2,1)}, u32[]{:S(2)}) copy-start(bf16[128,4,512]{2,0,1:T(8,128)(2,1)} %get-tuple-element.231) | copy-start | bytes 1572868 | tf_op jit(solution)/shard_map/while
  42.4 0.9 copy-start.1
  43.8 2.8 %copy-start.5 = (s32[128]{0:T(128)S(1)}, s32[128]{0:T(128)}, u32[]{:S(2)}) copy-start(s32[128]{0:T(128)} %get-tuple-element.256) | copy-start | bytes 1540 | tf_op jit(solution)/shard_map/while
  46.6 2.0 %copy-start.2 = (bf16[128,4,512]{2,0,1:T(8,128)(2,1)S(1)}, bf16[128,4,512]{2,0,1:T(8,128)(2,1)}, u32[]{:S(2)}) copy-start(bf16[128,4,512]{2,0,1:T(8,128)(2,1)} %get-tuple-element.231) | copy-start | bytes 1572868 | tf_op jit(solution)/shard_map/while
  47.8 0.9 copy-start.1
  49.2 3.1 %copy-start.5 = (s32[128]{0:T(128)S(1)}, s32[128]{0:T(128)}, u32[]{:S(2)}) copy-start(s32[128]{0:T(128)} %get-tuple-element.256) | copy-start | bytes 1540 | tf_op jit(solution)/shard_map/while
Sparse Core Ops, SparseCore 0:
  8.9 27.3 all-gather.3
  38.0 71.8 all-gather.5
  115.5 31.5 reduce-scatter.1
where the time goes:
time: 154 us
  waiting for transfers between devices  88.9 us (58%)
  blocking collectives  24.8 us (16%)
  matrix products  16.6 us (11%)
  between operations  13.9 us (9%)
  local copies, waits for them, and re-layouts  7.7 us (5%)
  other arithmetic  1.61 us (1%)
    all_gather x1, waiting for transfers between devices, shards(): lax.all_gather(w_out, 'ctx', axis=1, tiled=True)  55.7 us
    reduce_scatter x1, waiting for transfers between devices, shards(): lax.psum_scatter(partial_value.astype(jnp.bfloat16), 'head', scatter_dime...  31.7 us
    all_gather x1, blocking collectives, shards(): key_pos = lax.all_gather(token_pos, 'ctx', axis=0, tiled=True)  13.6 us
    all_gather x1, blocking collectives, shards(): features = lax.all_gather(q_latent, 'head', axis=1, tiled=True)  11.2 us
    dot_general x1, matrix products, shards(): jnp.dot(attention, lax.all_gather(w_out, 'ctx', axis=1, tiled=True), pref...  5.54 us
    dot_general x2, matrix products, attend(): jnp.einsum('hrk,kc->hrc', rounded, latent, preferred_element_type=jnp.flo...  5.47 us
  transfers between devices with their start and end apart: 3, of which 2 were waited for; matrix products, arithmetic and copies ran while one was open for 13% of the time, Pallas kernels for 0%

commit v1 on v0

v1 whole, which is shorter than its diff:
```python
import functools

import jax
import jax.numpy as jnp
from jax import lax
from jax.experimental import pallas as pl
from jax.experimental.pallas import tpu as pltpu
from jax.sharding import PartitionSpec as P

KVL = 512
NOPE = 128
ROPE = 64
VDIM = 128
LANES = 640

negative_fill = -1e30
softmax_scale = 0.135
rope_base = 10000.0
F32 = jnp.float32
BF16 = jnp.bfloat16
MESH = pl.DeviceIdType.MESH


def dot_t(a, b):
    return lax.dot_general(a, b, (((1,), (1,)), ((), ())), preferred_element_type=F32)


def kernel(
    n_c, n_h, heads, rows,
    qlat, lat, wq, wkv, wout, cos, sin, qpos,
    out,
    wq_v, wkv_v, w2, qbuf, latbuf, qa, score, prob, attbuf, pbuf, rsbuf, rbuf, zbuf,
    lsem, qs, qr, lzs, lps, latr, ws, wr, ats, atr, rss, rsr, zs, zr, os_, or_,
):
    n_z = n_c // 2
    piece = rows // n_h
    width = w2.shape[2]
    q_block = qbuf.shape[2]
    c = lax.axis_index("ctx")
    h = lax.axis_index("head")
    k = lax.rem(c, 2)
    z = lax.div(c, 2)
    partner = c + 1 - 2 * k
    z_of = [lax.rem(z + d, n_z) for d in range(n_z)]
    h_of = [lax.rem(h + e, n_h) for e in range(n_h)]
    c_of = [2 * zz + k for zz in z_of]

    def remote(src, dst, ssem, rsem, cc, hh):
        return pltpu.make_async_remote_copy(
            src_ref=src, dst_ref=dst, send_sem=ssem, recv_sem=rsem,
            device_id=(cc, hh), device_id_type=MESH,
        )

    def slot(cc):
        return latbuf.at[pl.ds(pl.multiple_of(cc * rows, rows), rows), :]

    barrier = pltpu.get_barrier_semaphore()
    for d in range(1, n_z):
        pl.semaphore_signal(barrier, inc=1, device_id=(c_of[d], h), device_id_type=MESH)
    for e in range(1, n_h):
        pl.semaphore_signal(barrier, inc=1, device_id=(c, h_of[e]), device_id_type=MESH)
    pl.semaphore_signal(barrier, inc=1, device_id=(partner, h), device_id_type=MESH)

    local = [
        pltpu.make_async_copy(qlat, qbuf.at[h], lsem.at[0]),
        pltpu.make_async_copy(wq, wq_v, lsem.at[1]),
        pltpu.make_async_copy(wkv, wkv_v, lsem.at[2]),
        pltpu.make_async_copy(lat, slot(c), lsem.at[3]),
        pltpu.make_async_copy(wout, w2.at[k], lsem.at[4]),
    ]
    for copy in local:
        copy.start()
    pl.semaphore_wait(barrier, n_z + n_h - 1)

    sends = []

    def send(*args):
        copy = remote(*args)
        copy.start()
        sends.append(copy)

    for e in range(1, n_h):
        send(qlat, qbuf.at[h], qs.at[e], qr.at[h], c, h_of[e])
    for d in range(n_z - 1, 0, -1):
        send(lat, slot(c), lzs.at[d], latr.at[c], c_of[d], h)
    send(lat, slot(c), lps.at[0], latr.at[c], partner, h)

    local[0].wait()
    local[1].wait()
    for e in range(1, n_h):
        remote(qlat, qbuf.at[h_of[e]], qs.at[e], qr.at[h_of[e]], c, h_of[e]).wait_recv()
    query = None
    for g in range(n_h):
        term = jnp.dot(qbuf[g], wq_v[g * q_block:(g + 1) * q_block, :], preferred_element_type=F32)
        query = term if query is None else query + term
    local[2].wait()
    for j in range(heads):
        base = j * (NOPE + ROPE)
        nope = query[:, base:base + NOPE].astype(BF16)
        main = dot_t(nope, wkv_v[:, j * 256:j * 256 + NOPE])
        lines = slice(j * rows, (j + 1) * rows)
        qa[lines, 0:KVL] = main.astype(BF16)
        rope = query[:, base + NOPE:base + NOPE + ROPE]
        half = ROPE // 2
        swapped = jnp.concatenate([rope[:, half:], rope[:, :half]], axis=1)
        rotated = rope * cos[...] + swapped * sin[...]
        qa[lines, KVL:LANES] = jnp.concatenate(
            [rotated.astype(BF16), jnp.zeros((rows, LANES - KVL - ROPE), BF16)], axis=1
        )

    for d in range(1, n_z):
        remote(lat, slot(c_of[d]), lzs.at[d], latr.at[c_of[d]], c_of[d], h).wait_recv()
        send(slot(c_of[d]), slot(c_of[d]), lps.at[d], latr.at[c_of[d]], partner, h)
    send(wout, w2.at[k], ws, wr, partner, h)
    local[3].wait()
    for d in range(n_z):
        cc = 2 * z_of[d] + 1 - k
        remote(lat, slot(cc), lps.at[d], latr.at[cc], partner, h).wait_recv()

    lane = lax.broadcasted_iota(jnp.int32, (8, 128), 1)
    pick = jnp.where(lane == ROPE, 64.0, jnp.where(lane == ROPE + 1, 1.0, 0.0)).astype(BF16)
    kpos = dot_t(pick, latbuf[:, KVL:LANES])[0:1, :]
    score[...] = dot_t(qa[...], latbuf[...])
    visible = kpos <= qpos[:, 0:1]
    sums = []
    for j in range(heads):
        lines = slice(j * rows, (j + 1) * rows)
        s = jnp.where(visible, score[lines, :] * softmax_scale, negative_fill)
        largest = jnp.max(s, axis=-1, keepdims=True)
        weights = jnp.where(visible, jnp.exp(s - largest), 0.0)
        sums.append(jnp.sum(weights, axis=-1, keepdims=True))
        prob[lines, :] = weights.astype(BF16)
    summed = jnp.dot(prob[...], latbuf[:, 0:KVL], preferred_element_type=F32)
    for j in range(heads):
        normed = (summed[j * rows:(j + 1) * rows, :] / sums[j]).astype(BF16)
        value = jnp.dot(normed, wkv_v[:, j * 256 + NOPE:(j + 1) * 256], preferred_element_type=F32)
        attbuf[z, :, j * VDIM:(j + 1) * VDIM] = value.astype(BF16)

    for d in range(n_z - 1, 0, -1):
        send(attbuf.at[z], attbuf.at[z], ats.at[d], atr.at[z], c_of[d], h)

    local[4].wait()
    remote(wout, w2.at[1 - k], ws, wr, partner, h).wait_recv()
    for d in range(n_z):
        zz = z_of[d]
        if d > 0:
            remote(attbuf.at[zz], attbuf.at[zz], ats.at[d], atr.at[zz], c_of[d], h).wait_recv()
        for m in range(2):
            part = jnp.dot(attbuf[zz], w2[m], preferred_element_type=F32).astype(BF16)
            for i in range(n_h):
                pbuf[zz, i, :, m * width:(m + 1) * width] = part[i * piece:(i + 1) * piece, :]
        for e in range(1, n_h):
            send(pbuf.at[zz, h_of[e]], rsbuf.at[zz, h], rss.at[d, e], rsr.at[zz, h], c, h_of[e])

    for d in range(n_z):
        zz = z_of[d]
        total = pbuf[zz, h].astype(F32)
        for e in range(1, n_h):
            hh = h_of[e]
            remote(pbuf.at[zz, hh], rsbuf.at[zz, hh], rss.at[d, e], rsr.at[zz, hh], c, hh).wait_recv()
            total = total + rsbuf[zz, hh].astype(F32)
        if d == 0:
            zbuf[z] = total.astype(BF16)
        else:
            rbuf[d] = total.astype(BF16)
            send(rbuf.at[d], zbuf.at[z], zs.at[d], zr.at[z], c_of[d], h)

    for e in range(1, n_h + 1):
        zz = h_of[e % n_h]

        @pl.when(zz != z)
        def _():
            remote(rbuf.at[0], zbuf.at[zz], zs.at[0], zr.at[zz], partner, h).wait_recv()

        if e < n_h:
            send(zbuf.at[zz], out.at[h], os_.at[e], or_.at[h], c, zz)
        else:
            out[h] = zbuf[h]
    for e in range(1, n_h):
        hh = h_of[e]
        remote(zbuf.at[0], out.at[hh], os_.at[e], or_.at[hh], c, hh).wait_recv()
    for copy in sends:
        copy.wait_send()


def shards(n_c, n_h, q_latent, latent_cache, w_q_up, w_kv_up, w_out, token_pos, start_offset):
    rows, q_block = q_latent.shape
    heads = w_q_up.shape[1] // (NOPE + ROPE)
    n_z = n_c // 2
    assert n_z == n_h
    keys = n_c * rows
    width = w_out.shape[1]
    piece = rows // n_h
    absolute = (token_pos + start_offset[0]).astype(F32)
    freqs = rope_base ** (-jnp.arange(ROPE // 2, dtype=F32) * 2.0 / ROPE)
    angle = absolute[:, None] * freqs[None, :]
    cosine, sine = jnp.cos(angle), jnp.sin(angle)
    cos = jnp.concatenate([cosine, cosine], axis=1)
    sin = jnp.concatenate([-sine, sine], axis=1)
    qpos = jnp.broadcast_to(token_pos.astype(F32)[:, None], (rows, 128))
    lat = jnp.concatenate(
        [
            latent_cache,
            (token_pos // 64).astype(BF16)[:, None],
            (token_pos % 64).astype(BF16)[:, None],
            jnp.zeros((rows, LANES - KVL - ROPE - 2), BF16),
        ],
        axis=1,
    )
    dma = pltpu.SemaphoreType.DMA
    anywhere = pl.BlockSpec(memory_space=pl.ANY)
    vmem = pl.BlockSpec(memory_space=pltpu.VMEM)
    result = pl.pallas_call(
        functools.partial(kernel, n_c, n_h, heads, rows),
        out_shape=jax.ShapeDtypeStruct((n_h, piece, 2 * width), BF16),
        in_specs=[anywhere] * 5 + [vmem] * 3,
        out_specs=vmem,
        scratch_shapes=[
            pltpu.VMEM(w_q_up.shape, BF16),
            pltpu.VMEM(w_kv_up.shape, BF16),
            pltpu.VMEM((2,) + w_out.shape, BF16),
            pltpu.VMEM((n_h, rows, q_block), BF16),
            pltpu.VMEM((keys, LANES), BF16),
            pltpu.VMEM((heads * rows, LANES), BF16),
            pltpu.VMEM((heads * rows, keys), F32),
            pltpu.VMEM((heads * rows, keys), BF16),
            pltpu.VMEM((n_z, rows, heads * VDIM), BF16),
            pltpu.VMEM((n_z, n_h, piece, 2 * width), BF16),
            pltpu.VMEM((n_z, n_h, piece, 2 * width), BF16),
            pltpu.VMEM((n_z, piece, 2 * width), BF16),
            pltpu.VMEM((n_z, piece, 2 * width), BF16),
            dma((5,)),
            dma((n_h,)), dma((n_h,)),
            dma((n_z,)), dma((n_z,)), dma((n_c,)),
            dma, dma,
            dma((n_z,)), dma((n_z,)),
            dma((n_z, n_h)), dma((n_z, n_h)),
            dma((n_z,)), dma((n_z,)),
            dma((n_h,)), dma((n_h,)),
        ],
        compiler_params=pltpu.CompilerParams(
            collective_id=0, has_side_effects=True, vmem_limit_bytes=60 * 1024 * 1024
        ),
        name="mla",
    )(q_latent, lat, w_q_up, w_kv_up, w_out, cos, sin, qpos)
    return result.reshape(rows, 2 * width)


def solution(mesh):
    in_specs = (
        P("ctx", "head"),
        P("ctx", None),
        P(None, "head"),
        P(None, "head"),
        P("head", "ctx"),
        P("ctx"),
        P(),
    )
    out_specs = P("ctx", "head")
    body = functools.partial(shards, mesh.shape["ctx"], mesh.shape["head"])
    return jax.shard_map(body, mesh=mesh, in_specs=in_specs, out_specs=out_specs, check_vma=False)
```

time: 154 us -> 70.9 us (0.46)
  waiting for transfers between devices: 88.9 us -> 0 us
  Pallas kernels: 0 us -> 63.4 us
  blocking collectives: 24.8 us -> 0 us
  matrix products: 16.6 us -> 0 us
  between operations: 13.9 us -> 0.68 us
  local copies, waits for them, and re-layouts: 7.7 us -> 3.94 us
    pallas_call x0 -> x1, Pallas kernels: none -> 63.4 us  [shards(): pl.pallas_call(functools.partial(kernel, n_c, n_h, heads, rows), out_shap...]
    all_gather x2 -> x0, waiting for transfers between devices: 55.7 us -> none  [the longest x1 55.7 us: shards(): lax.all_gather(w_out, 'ctx', axis=1, tiled=True)]
    reduce_scatter x1 -> x0, waiting for transfers between devices: 31.7 us -> none  [shards(): lax.psum_scatter(partial_value.astype(jnp.bfloat16), 'head', scatter_dime...]
    all_gather x2 -> x0, blocking collectives: 24.8 us -> none  [the longest x1 13.6 us: shards(): key_pos = lax.all_gather(token_pos, 'ctx', axis=0, tiled=True)]
    dot_general x10 -> x0, matrix products: 16.6 us -> none  [the longest x1 5.54 us: shards(): jnp.dot(attention, lax.all_gather(w_out, 'ctx', axis=1, tiled=True), pref...]
    reshape x2 -> x0, local copies, waits for them, and re-layouts: 2.45 us -> none  [the longest x1 2.44 us: shards(): block.reshape(count, 512, block.shape[1])]
    squeeze x2 -> x0, local copies, waits for them, and re-layouts: 2.32 us -> none  [shards(): lax.scan(scan_step, carry, (block.reshape(count, 512, block.shape[1]), ke...]
  transfers between devices with their start and end apart: 3 -> 0, of which waited for: 2 -> 0; matrix products, arithmetic and copies ran while one was open for 13% -> 0% of each run, Pallas kernels for 0% -> 0%
where the time goes in v1:
time: 70.9 us; the launch traced here: 70.6 us
  Pallas kernels  63.4 us (89%)
  local copies, waits for them, and re-layouts  3.94 us (6%)
  other arithmetic  2.58 us (4%)
    pallas_call x1, Pallas kernels, shards(): pl.pallas_call(functools.partial(kernel, n_c, n_h, heads, rows), out_shap...  63.4 us
    unnamed x2, local copies, waits for them, and re-layouts  2.88 us

profile of v1, /device:TPU:0, one launch (start us, length us, event | category | flops | bytes accessed | tf_op | source)
XLA Modules:
  0.0 70.6 jit_solution(4064060647950419495)
XLA Ops:
  0.7 0.1 pad.7.clone
  0.8 0.7 %fusion.3 = (f32[128]{0:T(128)S(1)}, bf16[128,1]{0,1:T(2,128)(2,1)S(1)}, bf16[128,1]{0,1:T(2,128)(2,1)S(1)}, f32[128]{0:T(128)S(1)}) fusion(s32[128]{0:T(128)} %param.12, s32[]{:T(128)} %bitcast.6), kind=kLoop, calls=%fused_computation.16 | loop fusion | flops 3072 | bytes 2052 | tf_op jit(solution)/shard_map/convert_element_type | solution.py:200
  1.5 0.1 copy.13
  1.6 0.1 copy.12
  1.8 0.7 %broadcast_in_dim.20.qpos = f32[128,128]{1,0:T(8,128)} broadcast(f32[128]{0:T(128)S(1)} %get-tuple-element.8), dimensions={0} | broadcast | bytes 66048 | tf_op jit(solution)/shard_map/broadcast_in_dim | solution.py:200
  2.5 1.1 %copy.11 = bf16[128,576]{1,0:T(8,128)(2,1)S(1)} copy(bf16[128,576]{0,1:T(8,128)(2,1)} %param.8) | data formatting | bytes 294912 | tf_op args[1]
  3.5 0.8 %maximum_maximum_fusion.lat = bf16[128,640]{1,0:T(8,128)(2,1)} fusion(bf16[128,1]{1,0:T(8,128)(2,1)S(1)} %copy.13, bf16[128,1]{1,0:T(8,128)(2,1)S(1)} %copy.12, bf16[128,576]{1,0:T(8,128)(2,1)S(1)} %copy.11, bf16[640]{0:T(1024)(128)(2,1)S(1)} %pad.7.clone), kind=kLoop, calls=%fused_computation | loop fusion | flops 655360 | bytes 313088 | tf_op jit(solution)/shard_map/concatenate | solution.py:201
  4.3 0.3 fusion
  4.6 0.8 %pad_maximum_fusion = (f32[128,64]{1,0:T(8,128)}, f32[128,64]{1,0:T(8,128)}) fusion(f32[128,32]{1,0:T(8,128)S(1)} %get-tuple-element.7, f32[128,32]{1,0:T(8,128)S(1)} %get-tuple-element.6, f32[128,32]{1,0:T(8,128)S(1)} %get-tuple-element.5), kind=kLoop, calls=%fused_computation.3 | loop fusion | flops 16384 | bytes 114688 | tf_op jit(solution)/shard_map/concatenate | solution.py:198
  5.4 63.4 %mla.1 = bf16[4,32,1792]{2,1,0:T(8,128)(2,1)} custom-call(bf16[128,384]{1,0:T(8,128)(2,1)} %qlat.1, bf16[128,640]{1,0:T(8,128)(2,1)} %maximum_maximum_fusion.lat, bf16[1536,768]{1,0:T(8,128)(2,1)} %wq.1, bf16[512,1024]{1,0:T(8,128)(2,1)} %wkv.1, bf16[512,896]{1,0:T(8,128)(2,1)} %wout.1, f32[128,64]{1,0:T(8,128)} %get-tuple-element.12.cos, ...), custom_call_target="tpu_custom_call" | custom-call | tf_op jit(solution)/shard_map/mla/pallas_call | solution.py:213
  68.8 1.8 %copy.17 = bf16[128,1792]{1,0:T(8,128)(2,1)} copy(bf16[128,1792]{1,0:T(8,128)(2,1)} %bitcast.7) | data formatting | bytes 917504
  (2 shorter events, 0.0 us)

commit v2 on v1

v2 whole, which is shorter than its diff:
```python
import functools

import jax
import jax.numpy as jnp
from jax import lax
from jax.experimental import pallas as pl
from jax.experimental.pallas import tpu as pltpu
from jax.sharding import PartitionSpec as P

KVL = 512
NOPE = 128
ROPE = 64
VDIM = 128
LANES = KVL + ROPE

negative_fill = -1e30
softmax_scale = 0.135
rope_base = 10000.0
F32 = jnp.float32
BF16 = jnp.bfloat16
MESH = pl.DeviceIdType.MESH


def dot_t(a, b):
    return lax.dot_general(a, b, (((1,), (1,)), ((), ())), preferred_element_type=F32)


def kernel(
    n_c, n_h, heads, rows,
    qlat, lat, wq, wkv, wout, cos, sin, kpos, qpos,
    out,
    wq_v, wkv_v, w2, qbuf, latbuf, posbuf, qa, score, prob, attbuf,
    pa, ra, ta, qa2, pb, rb, tb, qb2, rbuf, zbuf,
    lsem, qs, qr, lzs, lps, latr, pzs, pzr, pps, ppr, ws, wr, ats, atr,
    sa1, va1, sa2, va2, sb1, vb1, sb2, vb2, zs, zr, os_, or_,
):
    n_z = n_c // 2
    piece = rows // n_h
    n_lo = n_h // 2
    width = w2.shape[2]
    q_block = qbuf.shape[2]
    c = lax.axis_index("ctx")
    h = lax.axis_index("head")
    k = lax.rem(c, 2)
    z = lax.div(c, 2)
    partner = c + 1 - 2 * k
    z_of = [lax.rem(z + d, n_z) for d in range(n_z)]
    h_of = [lax.rem(h + e, n_h) for e in range(n_h)]
    hi, lo = lax.div(h, n_lo), lax.rem(h, n_lo)
    lo_of = [lax.rem(lo + e, n_lo) for e in range(n_lo)]
    c_of = [2 * zz + k for zz in z_of]

    def remote(src, dst, ssem, rsem, cc, hh):
        return pltpu.make_async_remote_copy(
            src_ref=src, dst_ref=dst, send_sem=ssem, recv_sem=rsem,
            device_id=(cc, hh), device_id_type=MESH,
        )

    def slot(cc):
        return latbuf.at[cc]

    barrier = pltpu.get_barrier_semaphore()
    for d in range(1, n_z):
        pl.semaphore_signal(barrier, inc=1, device_id=(c_of[d], h), device_id_type=MESH)
    for e in range(1, n_h):
        pl.semaphore_signal(barrier, inc=1, device_id=(c, h_of[e]), device_id_type=MESH)
    pl.semaphore_signal(barrier, inc=1, device_id=(partner, h), device_id_type=MESH)

    local = [
        pltpu.make_async_copy(qlat, qbuf.at[h], lsem.at[0]),
        pltpu.make_async_copy(wq, wq_v, lsem.at[1]),
        pltpu.make_async_copy(wkv, wkv_v, lsem.at[2]),
        pltpu.make_async_copy(lat, slot(c), lsem.at[3]),
        pltpu.make_async_copy(wout, w2.at[k], lsem.at[4]),
    ]
    for copy in local:
        copy.start()
    pl.semaphore_wait(barrier, n_z + n_h - 1)

    sends = []

    def send(*args):
        copy = remote(*args)
        copy.start()
        sends.append(copy)

    for e in range(1, n_h):
        send(qlat, qbuf.at[h], qs.at[e], qr.at[h], c, h_of[e])
    for d in range(n_z - 1, 0, -1):
        send(lat, slot(c), lzs.at[d], latr.at[c], c_of[d], h)
    send(lat, slot(c), lps.at[0], latr.at[c], partner, h)
    posbuf[k, z] = kpos[...]
    for d in range(1, n_z):
        send(kpos, posbuf.at[k, z], pzs.at[d], pzr.at[z], c_of[d], h)

    local[0].wait()
    local[1].wait()
    for e in range(1, n_h):
        remote(qlat, qbuf.at[h_of[e]], qs.at[e], qr.at[h_of[e]], c, h_of[e]).wait_recv()
    query = None
    for g in range(n_h):
        term = jnp.dot(qbuf[g], wq_v[g * q_block:(g + 1) * q_block, :], preferred_element_type=F32)
        query = term if query is None else query + term
    local[2].wait()
    for j in range(heads):
        base = j * (NOPE + ROPE)
        nope = query[:, base:base + NOPE].astype(BF16)
        main = dot_t(nope, wkv_v[:, j * 256:j * 256 + NOPE])
        lines = slice(j * rows, (j + 1) * rows)
        qa[lines, 0:KVL] = main.astype(BF16)
        rope = query[:, base + NOPE:base + NOPE + ROPE]
        half = ROPE // 2
        swapped = jnp.concatenate([rope[:, half:], rope[:, :half]], axis=1)
        rotated = rope * cos[...] + swapped * sin[...]
        qa[lines, KVL:LANES] = rotated.astype(BF16)

    for d in range(1, n_z):
        remote(lat, slot(c_of[d]), lzs.at[d], latr.at[c_of[d]], c_of[d], h).wait_recv()
        send(slot(c_of[d]), slot(c_of[d]), lps.at[d], latr.at[c_of[d]], partner, h)
    for d in range(1, n_z):
        remote(kpos, posbuf.at[k, z_of[d]], pzs.at[d], pzr.at[z_of[d]], c_of[d], h).wait_recv()
    send(posbuf.at[k], posbuf.at[k], pps, ppr, partner, h)
    send(wout, w2.at[k], ws, wr, partner, h)
    local[3].wait()
    for d in range(n_z):
        cc = 2 * z_of[d] + 1 - k
        remote(lat, slot(cc), lps.at[d], latr.at[cc], partner, h).wait_recv()

    remote(posbuf.at[1 - k], posbuf.at[1 - k], pps, ppr, partner, h).wait_recv()
    key_pos = jnp.concatenate([posbuf[cc % 2, cc // 2, 0:1, :] for cc in range(n_c)], axis=1)
    latents = jnp.concatenate([latbuf[cc] for cc in range(n_c)], axis=1)
    score[...] = jnp.dot(qa[...], latents, preferred_element_type=F32)
    visible = key_pos <= qpos[:, 0:1]
    sums = []
    for j in range(heads):
        lines = slice(j * rows, (j + 1) * rows)
        s = jnp.where(visible, score[lines, :] * softmax_scale, negative_fill)
        largest = jnp.max(s, axis=-1, keepdims=True)
        weights = jnp.where(visible, jnp.exp(s - largest), 0.0)
        sums.append(jnp.sum(weights, axis=-1, keepdims=True))
        prob[lines, :] = weights.astype(BF16)
    summed = dot_t(prob[...], latents[0:KVL, :])
    for j in range(heads):
        normed = (summed[j * rows:(j + 1) * rows, :] / sums[j]).astype(BF16)
        value = jnp.dot(normed, wkv_v[:, j * 256 + NOPE:(j + 1) * 256], preferred_element_type=F32)
        attbuf[z, :, j * VDIM:(j + 1) * VDIM] = value.astype(BF16)

    for d in range(n_z - 1, 0, -1):
        send(attbuf.at[z], attbuf.at[z], ats.at[d], atr.at[z], c_of[d], h)

    local[4].wait()
    remote(wout, w2.at[1 - k], ws, wr, partner, h).wait_recv()

    def project(d):
        zz = z_of[d]
        if d > 0:
            remote(attbuf.at[zz], attbuf.at[zz], ats.at[d], atr.at[zz], c_of[d], h).wait_recv()
        part = jnp.dot(attbuf[zz], w2[0], preferred_element_type=F32).astype(BF16)
        for i in range(n_h):
            pa[d, i % n_lo, i // n_lo] = part[i * piece:(i + 1) * piece, :]
        for e in range(1, n_lo):
            send(pa.at[d, lo_of[e]], ra.at[d, lo], sa1.at[d, e], va1.at[d, lo], c, hi * n_lo + lo_of[e])
        part = jnp.dot(attbuf[zz], w2[1], preferred_element_type=F32).astype(BF16)
        for i in range(n_h):
            pb[d, i // n_lo, i % n_lo] = part[i * piece:(i + 1) * piece, :]
        send(pb.at[d, 1 - hi], rb.at[d], sb1.at[d], vb1.at[d], c, (1 - hi) * n_lo + lo)

    def second(d):
        total = pa[d, lo].astype(F32)
        for e in range(1, n_lo):
            ll = lo_of[e]
            remote(pa.at[d, ll], ra.at[d, ll], sa1.at[d, e], va1.at[d, ll], c, hi * n_lo + ll).wait_recv()
            total = total + ra[d, ll].astype(F32)
        ta[d] = total.astype(BF16)
        send(ta.at[d, 1 - hi], qa2.at[d], sa2.at[d], va2.at[d], c, (1 - hi) * n_lo + lo)
        remote(pb.at[d, hi], rb.at[d], sb1.at[d], vb1.at[d], c, (1 - hi) * n_lo + lo).wait_recv()
        tb[d] = (pb[d, hi].astype(F32) + rb[d].astype(F32)).astype(BF16)
        for e in range(1, n_lo):
            send(tb.at[d, lo_of[e]], qb2.at[d, lo], sb2.at[d, e], vb2.at[d, lo], c, hi * n_lo + lo_of[e])

    def third(d):
        remote(ta.at[d, hi], qa2.at[d], sa2.at[d], va2.at[d], c, (1 - hi) * n_lo + lo).wait_recv()
        first = (ta[d, hi].astype(F32) + qa2[d].astype(F32)).astype(BF16)
        total = tb[d, lo].astype(F32)
        for e in range(1, n_lo):
            ll = lo_of[e]
            remote(tb.at[d, ll], qb2.at[d, ll], sb2.at[d, e], vb2.at[d, ll], c, hi * n_lo + ll).wait_recv()
            total = total + qb2[d, ll].astype(F32)
        if d == 0:
            zbuf[z, :, 0:width] = first
            zbuf[z, :, width:] = total.astype(BF16)
        else:
            rbuf[d, :, 0:width] = first
            rbuf[d, :, width:] = total.astype(BF16)
            send(rbuf.at[d], zbuf.at[z], zs.at[d], zr.at[z], c_of[d], h)

    def deliver(d):
        zz = z_of[(n_z - d) % n_z]
        if d > 0:
            remote(rbuf.at[0], zbuf.at[zz], zs.at[0], zr.at[zz], partner, h).wait_recv()

        @pl.when(zz != h)
        def _():
            remote(zbuf.at[zz], out.at[h], os_.at[d], or_.at[h], c, zz).start()

        @pl.when(zz == h)
        def _():
            out[h] = zbuf[zz]

    def delivered(d):
        zz = z_of[(n_z - d) % n_z]

        @pl.when(zz != h)
        def _():
            remote(zbuf.at[zz], out.at[h], os_.at[d], or_.at[h], c, zz).wait_send()

    for d in range(n_z + 3):
        if d < n_z:
            project(d)
        if 1 <= d <= n_z:
            second(d - 1)
        if 2 <= d <= n_z + 1:
            third(d - 2)
        if d >= 3:
            deliver(d - 3)
    for e in range(1, n_h):
        hh = h_of[e]
        remote(zbuf.at[0], out.at[hh], os_.at[0], or_.at[hh], c, hh).wait_recv()
    for d in range(n_z):
        delivered(d)
    for copy in sends:
        copy.wait_send()


def shards(n_c, n_h, q_latent, latent_cache, w_q_up, w_kv_up, w_out, token_pos, start_offset):
    rows, q_block = q_latent.shape
    heads = w_q_up.shape[1] // (NOPE + ROPE)
    n_z, n_lo = n_c // 2, n_h // 2
    assert n_z == n_h
    keys = n_c * rows
    width = w_out.shape[1]
    piece = rows // n_h
    absolute = (token_pos + start_offset[0]).astype(F32)
    freqs = rope_base ** (-jnp.arange(ROPE // 2, dtype=F32) * 2.0 / ROPE)
    angle = absolute[:, None] * freqs[None, :]
    cosine, sine = jnp.cos(angle), jnp.sin(angle)
    cos = jnp.concatenate([cosine, cosine], axis=1)
    sin = jnp.concatenate([-sine, sine], axis=1)
    qpos = jnp.broadcast_to(token_pos.astype(F32)[:, None], (rows, 128))
    kpos = jnp.broadcast_to(token_pos.astype(F32)[None, :], (8, rows))
    dma = pltpu.SemaphoreType.DMA
    anywhere = pl.BlockSpec(memory_space=pltpu.HBM)
    vmem = pl.BlockSpec(memory_space=pltpu.VMEM)
    result = pl.pallas_call(
        functools.partial(kernel, n_c, n_h, heads, rows),
        out_shape=jax.ShapeDtypeStruct((n_h, piece, 2 * width), BF16),
        in_specs=[anywhere] * 5 + [vmem] * 4,
        out_specs=vmem,
        scratch_shapes=[
            pltpu.VMEM(w_q_up.shape, BF16),
            pltpu.VMEM(w_kv_up.shape, BF16),
            pltpu.VMEM((2,) + w_out.shape, BF16),
            pltpu.VMEM((n_h, rows, q_block), BF16),
            pltpu.VMEM((n_c, LANES, rows), BF16),
            pltpu.VMEM((2, n_z, 8, rows), F32),
            pltpu.VMEM((heads * rows, LANES), BF16),
            pltpu.VMEM((heads * rows, keys), F32),
            pltpu.VMEM((heads * rows, keys), BF16),
            pltpu.VMEM((n_z, rows, heads * VDIM), BF16),
            pltpu.VMEM((n_z, n_lo, 2, piece, width), BF16),
            pltpu.VMEM((n_z, n_lo, 2, piece, width), BF16),
            pltpu.VMEM((n_z, 2, piece, width), BF16),
            pltpu.VMEM((n_z, piece, width), BF16),
            pltpu.VMEM((n_z, 2, n_lo, piece, width), BF16),
            pltpu.VMEM((n_z, n_lo, piece, width), BF16),
            pltpu.VMEM((n_z, n_lo, piece, width), BF16),
            pltpu.VMEM((n_z, n_lo, piece, width), BF16),
            pltpu.VMEM((n_z, piece, 2 * width), BF16),
            pltpu.VMEM((n_z, piece, 2 * width), BF16),
            dma((5,)),
            dma((n_h,)), dma((n_h,)),
            dma((n_z,)), dma((n_z,)), dma((n_c,)),
            dma((n_z,)), dma((n_z,)), dma, dma,
            dma, dma,
            dma((n_z,)), dma((n_z,)),
            dma((n_z, n_lo)), dma((n_z, n_lo)), dma((n_z,)), dma((n_z,)),
            dma((n_z,)), dma((n_z,)), dma((n_z, n_lo)), dma((n_z, n_lo)),
            dma((n_z,)), dma((n_z,)),
            dma((n_z,)), dma((n_h,)),
        ],
        compiler_params=pltpu.CompilerParams(
            collective_id=0, has_side_effects=True, vmem_limit_bytes=67043328 - (768 << 10)
        ),
        name="mla",
    )(q_latent, latent_cache.T, w_q_up, w_kv_up, w_out, cos, sin, kpos, qpos)
    return result.reshape(rows, 2 * width)


def solution(mesh):
    in_specs = (
        P("ctx", "head"),
        P("ctx", None),
        P(None, "head"),
        P(None, "head"),
        P("head", "ctx"),
        P("ctx"),
        P(),
    )
    out_specs = P("ctx", "head")
    body = functools.partial(shards, mesh.shape["ctx"], mesh.shape["head"])
    return jax.shard_map(body, mesh=mesh, in_specs=in_specs, out_specs=out_specs, check_vma=False)
```

time: 70.9 us -> 65.3 us (0.921)
  Pallas kernels: 63.4 us -> 58.8 us
  local copies, waits for them, and re-layouts: 3.94 us -> 3.11 us
  other arithmetic: 2.58 us -> 1.81 us
    pallas_call x1, Pallas kernels: 63.4 us -> 58.8 us  [shards(): pl.pallas_call(functools.partial(kernel, n_c, n_h, heads, rows), out_shap...]
    unnamed x2 -> x1, local copies, waits for them, and re-layouts: 2.88 us -> 1.82 us
    concatenate x1 -> x0, other arithmetic: 0.76 us -> none  [shards(): jnp.concatenate([latent_cache, (token_pos // 64).astype(BF16)[:, None], (...]
where the time goes in v2:
time: 65.3 us; the launch traced here: 64.4 us
  Pallas kernels  58.8 us (90%)
  local copies, waits for them, and re-layouts  3.11 us (5%)
  other arithmetic  1.81 us (3%)
  between operations  0.67 us (1%)
    pallas_call x1, Pallas kernels, shards(): pl.pallas_call(functools.partial(kernel, n_c, n_h, heads, rows), out_shap...  58.8 us
    unnamed x1, local copies, waits for them, and re-layouts  1.82 us

profile of v2, /device:TPU:0, one launch (start us, length us, event | category | flops | bytes accessed | tf_op | source)
XLA Modules:
  0.0 64.4 jit_solution(5078235306690744189)
XLA Ops:
  0.7 0.7 %fusion.1 = (f32[128]{0:T(128)S(1)}, f32[128]{0:T(128)S(1)}) fusion(s32[128]{0:T(128)} %param.12, s32[]{:T(128)} %bitcast.3), kind=kLoop, calls=%fused_computation.7 | loop fusion | flops 384 | bytes 1540 | tf_op jit(solution)/shard_map/convert_element_type | solution.py:250
  1.4 0.6 broadcast_in_dim.4.kpos
  2.0 0.7 %broadcast_in_dim.5.qpos = f32[128,128]{1,0:T(8,128)} broadcast(f32[128]{0:T(128)S(1)} %get-tuple-element.8), dimensions={0} | broadcast | bytes 66048 | tf_op jit(solution)/shard_map/broadcast_in_dim | solution.py:249
  2.7 0.3 fusion
  3.0 0.8 %pad_maximum_fusion = (f32[128,64]{1,0:T(8,128)}, f32[128,64]{1,0:T(8,128)}) fusion(f32[128,32]{1,0:T(8,128)S(1)} %get-tuple-element.7, f32[128,32]{1,0:T(8,128)S(1)} %get-tuple-element.6, f32[128,32]{1,0:T(8,128)S(1)} %get-tuple-element.5), kind=kLoop, calls=%fused_computation.2 | loop fusion | flops 16384 | bytes 114688 | tf_op jit(solution)/shard_map/concatenate | solution.py:247
  3.8 58.8 %mla.1 = bf16[4,32,1792]{2,1,0:T(8,128)(2,1)} custom-call(bf16[128,384]{1,0:T(8,128)(2,1)} %qlat.1, bf16[576,128]{1,0:T(8,128)(2,1)} %bitcast.5, bf16[1536,768]{1,0:T(8,128)(2,1)} %wq.1, bf16[512,1024]{1,0:T(8,128)(2,1)} %wkv.1, bf16[512,896]{1,0:T(8,128)(2,1)} %wout.1, f32[128,64]{1,0:T(8,128)} %get-tuple-element.10.cos, f32[128,64]{1,0:T(8,128)} %get-tuple-element.11.sin, ...), custom_call_target="tpu_custom_call" | custom-call | tf_op jit(solution)/shard_map/mla/pallas_call | solution.py:254
  62.6 1.8 %copy.11 = bf16[128,1792]{1,0:T(8,128)(2,1)} copy(bf16[128,1792]{1,0:T(8,128)(2,1)} %bitcast.4) | data formatting | bytes 917504
  (1 shorter events, 0.0 us)

commit v3 on v2

--- a/solution.py
+++ b/solution.py
@@ -27,11 +27,11 @@
 
 def kernel(
     n_c, n_h, heads, rows,
-    qlat, lat, wq, wkv, wout, cos, sin, kpos, qpos,
+    qlat, lat, wq, wkv, wout, cos, sin, kpos,
     out,
     wq_v, wkv_v, w2, qbuf, latbuf, posbuf, qa, score, prob, attbuf,
     pa, ra, ta, qa2, pb, rb, tb, qb2, rbuf, zbuf,
-    lsem, qs, qr, lzs, lps, latr, pzs, pzr, pps, ppr, ws, wr, ats, atr,
+    lsem, qs, qr, lzs, lps, latr, xzs, xzr, xps, xpr, pzs, pzr, pps, ppr, ws, wr, ats, atr,
     sa1, va1, sa2, va2, sb1, vb1, sb2, vb2, zs, zr, os_, or_,
 ):
     n_z = n_c // 2
@@ -77,6 +77,12 @@
         copy.start()
     pl.semaphore_wait(barrier, n_z + n_h - 1)
 
+    third_rows = LANES // 3
+    odd = lax.rem(lo, 2)
+    pair = hi * n_lo + lo + 1 - 2 * odd
+    mine = pl.ds(pl.multiple_of(odd * third_rows, third_rows), third_rows)
+    other = pl.ds(pl.multiple_of((1 - odd) * third_rows, third_rows), third_rows)
+    both = pl.ds(2 * third_rows, third_rows)
     sends = []
 
     def send(*args):
@@ -87,11 +93,18 @@
     for e in range(1, n_h):
         send(qlat, qbuf.at[h], qs.at[e], qr.at[h], c, h_of[e])
     for d in range(n_z - 1, 0, -1):
-        send(lat, slot(c), lzs.at[d], latr.at[c], c_of[d], h)
+        send(lat.at[mine, :], latbuf.at[c, mine, :], xzs.at[d], xzr.at[z], c_of[d], h)
+    for d in range(n_z - 1, 0, -1):
+        send(lat.at[both, :], latbuf.at[c, both, :], lzs.at[d], latr.at[c], c_of[d], h)
     send(lat, slot(c), lps.at[0], latr.at[c], partner, h)
     posbuf[k, z] = kpos[...]
     for d in range(1, n_z):
         send(kpos, posbuf.at[k, z], pzs.at[d], pzr.at[z], c_of[d], h)
+
+    for d in range(1, n_z):
+        cc = c_of[d]
+        remote(lat.at[mine, :], latbuf.at[cc, mine, :], xzs.at[d], xzr.at[z_of[d]], cc, h).wait_recv()
+        send(latbuf.at[cc, mine, :], latbuf.at[cc, mine, :], xps.at[d], xpr.at[z_of[d]], c, pair)
 
     local[0].wait()
     local[1].wait()
@@ -115,7 +128,11 @@
         qa[lines, KVL:LANES] = rotated.astype(BF16)
 
     for d in range(1, n_z):
-        remote(lat, slot(c_of[d]), lzs.at[d], latr.at[c_of[d]], c_of[d], h).wait_recv()
+        cc = c_of[d]
+        remote(lat.at[both, :], latbuf.at[cc, both, :], lzs.at[d], latr.at[cc], cc, h).wait_recv()
+        remote(
+            latbuf.at[cc, other, :], latbuf.at[cc, other, :], xps.at[d], xpr.at[z_of[d]], c, pair
+        ).wait_recv()
         send(slot(c_of[d]), slot(c_of[d]), lps.at[d], latr.at[c_of[d]], partner, h)
     for d in range(1, n_z):
         remote(kpos, posbuf.at[k, z_of[d]], pzs.at[d], pzr.at[z_of[d]], c_of[d], h).wait_recv()
@@ -130,7 +147,7 @@
     key_pos = jnp.concatenate([posbuf[cc % 2, cc // 2, 0:1, :] for cc in range(n_c)], axis=1)
     latents = jnp.concatenate([latbuf[cc] for cc in range(n_c)], axis=1)
     score[...] = jnp.dot(qa[...], latents, preferred_element_type=F32)
-    visible = key_pos <= qpos[:, 0:1]
+    visible = key_pos <= jnp.transpose(kpos[...])[:, 0:1]
     sums = []
     for j in range(heads):
         lines = slice(j * rows, (j + 1) * rows)
@@ -246,7 +263,6 @@
     cosine, sine = jnp.cos(angle), jnp.sin(angle)
     cos = jnp.concatenate([cosine, cosine], axis=1)
     sin = jnp.concatenate([-sine, sine], axis=1)
-    qpos = jnp.broadcast_to(token_pos.astype(F32)[:, None], (rows, 128))
     kpos = jnp.broadcast_to(token_pos.astype(F32)[None, :], (8, rows))
     dma = pltpu.SemaphoreType.DMA
     anywhere = pl.BlockSpec(memory_space=pltpu.HBM)
@@ -254,7 +270,7 @@
     result = pl.pallas_call(
         functools.partial(kernel, n_c, n_h, heads, rows),
         out_shape=jax.ShapeDtypeStruct((n_h, piece, 2 * width), BF16),
-        in_specs=[anywhere] * 5 + [vmem] * 4,
+        in_specs=[anywhere] * 5 + [vmem] * 3,
         out_specs=vmem,
         scratch_shapes=[
             pltpu.VMEM(w_q_up.shape, BF16),
@@ -280,6 +296,7 @@
             dma((5,)),
             dma((n_h,)), dma((n_h,)),
             dma((n_z,)), dma((n_z,)), dma((n_c,)),
+            dma((n_z,)), dma((n_z,)), dma((n_z,)), dma((n_z,)),
             dma((n_z,)), dma((n_z,)), dma, dma,
             dma, dma,
             dma((n_z,)), dma((n_z,)),
@@ -292,7 +309,7 @@
             collective_id=0, has_side_effects=True, vmem_limit_bytes=67043328 - (768 << 10)
         ),
         name="mla",
-    )(q_latent, latent_cache.T, w_q_up, w_kv_up, w_out, cos, sin, kpos, qpos)
+    )(q_latent, latent_cache.T, w_q_up, w_kv_up, w_out, cos, sin, kpos)
     return result.reshape(rows, 2 * width)
 
 

time: 65.3 us -> 63 us (0.965)
  the two profiles are of different devices: /device:TPU:0 before, /device:TPU:24 now
where the time goes in v3:
time: 63 us; the launch traced here: 62.8 us
  Pallas kernels  57.9 us (92%)
  local copies, waits for them, and re-layouts  2.41 us (4%)
  other arithmetic  1.81 us (3%)
  between operations  0.67 us (1%)
    pallas_call x1, Pallas kernels, shards(): pl.pallas_call(functools.partial(kernel, n_c, n_h, heads, rows), out_shap...  57.9 us
    unnamed x1, local copies, waits for them, and re-layouts  1.82 us

profile of v3, /device:TPU:24, one launch (start us, length us, event | category | flops | bytes accessed | tf_op | source)
XLA Modules:
  0.0 62.8 jit_solution(17611043971957233660)
XLA Ops:
  0.7 0.7 %fusion.1 = (f32[128]{0:T(128)S(1)}, f32[128]{0:T(128)S(1)}) fusion(s32[128]{0:T(128)} %param.12, s32[]{:T(128)} %bitcast.3), kind=kLoop, calls=%fused_computation.7 | loop fusion | flops 384 | bytes 1540 | tf_op jit(solution)/shard_map/convert_element_type | solution.py:266
  1.4 0.6 broadcast_in_dim.2.kpos
  2.0 0.3 fusion
  2.3 0.8 %pad_maximum_fusion = (f32[128,64]{1,0:T(8,128)}, f32[128,64]{1,0:T(8,128)}) fusion(f32[128,32]{1,0:T(8,128)S(1)} %get-tuple-element.7, f32[128,32]{1,0:T(8,128)S(1)} %get-tuple-element.6, f32[128,32]{1,0:T(8,128)S(1)} %get-tuple-element.5), kind=kLoop, calls=%fused_computation.2 | loop fusion | flops 16384 | bytes 114688 | tf_op jit(solution)/shard_map/concatenate | solution.py:264
  3.1 57.9 %mla.1 = bf16[4,32,1792]{2,1,0:T(8,128)(2,1)} custom-call(bf16[128,384]{1,0:T(8,128)(2,1)} %qlat.1, bf16[576,128]{1,0:T(8,128)(2,1)} %bitcast.5, bf16[1536,768]{1,0:T(8,128)(2,1)} %wq.1, bf16[512,1024]{1,0:T(8,128)(2,1)} %wkv.1, bf16[512,896]{1,0:T(8,128)(2,1)} %wout.1, f32[128,64]{1,0:T(8,128)} %get-tuple-element.10.cos, f32[128,64]{1,0:T(8,128)} %get-tuple-element.11.sin, ...), custom_call_target="tpu_custom_call" | custom-call | tf_op jit(solution)/shard_map/mla/pallas_call | solution.py:270
  61.0 1.8 %copy.11 = bf16[128,1792]{1,0:T(8,128)(2,1)} copy(bf16[128,1792]{1,0:T(8,128)(2,1)} %bitcast.4) | data formatting | bytes 917504
  (1 shorter events, 0.0 us)
